TPU v7x, 256 devices: a whole 4x4x8 slice. The times are simulated.
256 devices in a mesh: rows: 4 (over y), past: 64 (over x, z, core).
Axes of the slice: x: 4, y: 4, z: 8, core: 2. Of those that a mesh axis runs over, the one named last changes fastest.
Arguments:
- tile_left: float32 [4, 64, 1024, 128], P('rows', 'past'), may hold values from -0.0625 to 0.0625
- tile_right: float32 [4, 64, 1024, 128], P('rows', 'past'), may hold values from -0.1875 to 0.1875
- diag_left: float32 [64, 1024, 128], P('past', 'rows'), may hold values from -6 to 6
- diag_right: float32 [64, 1024, 128], P('past', 'rows'), may hold values from -0.1875 to 0.1875
- present: int32 [4, 64], P('rows', 'past'), may hold values 0 or 1
- old_left: float32 [4, 1024, 128], P('rows'), may hold values from -6 to 6
- old_right: float32 [4, 1024, 128], P('rows'), may hold values from -0.1875 to 0.1875
- start: float32 [4, 1024, 128], P('rows'), may hold values from -6 to 6
Outputs:
- left: float32 [4, 1024, 128], P('rows')
- right: float32 [4, 1024, 128], P('rows')
Inputs may be any that keep to these rules, and one draw needn't show every extreme that they name: present is 1 exactly where the past tile of that tile row and panel is listed.
All inputs are finite; a program needn't handle non-finite values. No bound on the sum of `present` on one device may be relied on, other than what follows from the above.
Results may differ from a plain program's by a relative error of at most 0.00026.
Values sent between devices are 32-bit elements; how exact they have to be, the bound alone decides.
No kernel may reach another device: no remote copies, remote signals or barrier semaphores. Data moves between devices by JAX's collectives and lax.ppermute only.
A program may use at most 64 MiB of HBM per device.

v0:
```python
import math
import jax
import jax.numpy as jnp
from jax import lax
from jax.sharding import PartitionSpec as P

B = 1024
ITERS = 3
HIGH = lax.Precision.HIGHEST


def lower_inverse(gram):
    lower = jnp.linalg.cholesky(gram)
    ident = jnp.eye(gram.shape[-1], dtype=jnp.float32)
    return jax.vmap(lambda one: jax.scipy.linalg.solve_triangular(one, ident, lower=True))(lower)


def shards(tile_left, tile_right, diag_left, diag_right, present, old_left, old_right, start):
    diag_left, diag_right = (
        lax.all_gather(diag_left, "rows", axis=1, tiled=True),
        lax.all_gather(diag_right, "rows", axis=1, tiled=True),
    )
    weights = present.astype(jnp.float32)
    coupling = (
        jnp.einsum("ipbr,pbs->iprs", tile_right, diag_right, precision=HIGH)
        * weights[:, :, None, None]
    )

    def forward(block):
        inner = jnp.einsum("pbs,ibt->ipst", diag_left, block, precision=HIGH)
        middle = jnp.einsum("iprs,ipst->iprt", coupling, inner, precision=HIGH)
        summed = jnp.einsum("ipbr,iprt->ibt", tile_left, middle, precision=HIGH)
        small = jnp.einsum("ibr,ibt->irt", old_right, block, precision=HIGH)
        return (-summed, old_left, small)

    def backward(block):
        inner = jnp.einsum("ipbr,ibt->iprt", tile_left, block, precision=HIGH)
        middle = jnp.einsum("iprs,iprt->ipst", coupling, inner, precision=HIGH)
        summed = jnp.einsum("pbs,ipst->ibt", diag_left, middle, precision=HIGH)
        small = jnp.einsum("ibr,ibt->irt", old_left, block, precision=HIGH)
        return (-summed, old_right, small)

    def combine(terms, orthogonal):
        partial_value, vectors, small = terms
        total = lax.psum(partial_value, "past")
        total = total + jnp.einsum("ibr,irt->ibt", vectors, small, precision=HIGH)
        if orthogonal:
            gram = jnp.einsum("ibr,ibs->irs", total, total, precision=HIGH)
            total = jnp.einsum("ibr,isr->ibs", total, lower_inverse(gram), precision=HIGH)
        return total

    basis = combine(forward(start), True)
    for sweep in range(ITERS):
        basis = combine(forward(combine(backward(basis), True)), True)
    right = combine(backward(basis), False)
    return (basis * math.sqrt(B), right)


def solution(mesh):
    placed = (
        P("rows", "past", None, None),
        P("rows", "past", None, None),
        P("past", "rows", None),
        P("past", "rows", None),
        P("rows", "past"),
        P("rows", None, None),
        P("rows", None, None),
        P("rows", None, None),
    )
    return jax.shard_map(
        shards,
        mesh=mesh,
        in_specs=placed,
        out_specs=(P("rows", None, None), P("rows", None, None)),
        check_vma=False,
    )
```

profile of v0, /device:TPU:8, one launch (start us, length us, event | category | flops | bytes accessed | tf_op | source)
XLA Modules:
  0.0 1704.0 jit_solution(11065047977644913522)
XLA Ops:
  7.9 14.0 all_gather.7
  21.9 12.8 all_gather.6
  34.7 1.0 convolution_bitcast_fusion.11
  37.1 1.5 fusion.7
  40.6 184.5 %all-reduce.9.cloned.1.call-done = f32[1,1024,128]{1,2,0:T(8,128)} async-done(((f32[1,1024,128]{1,2,0:T(8,128)}), f32[1,1024,128]{1,2,0:T(8,128)}) %all-reduce.9.cloned.1.call-update) | async-done | bytes 524304 | tf_op jit(solution)/shard_map/psum | solution.py:45
  225.1 1.7 fusion.9
  227.5 11.7 custom-call.18
  240.5 9.8 custom-call.19
  251.6 1.0 fusion.57
  252.9 1.5 fusion.6
  254.6 1.0 fusion.33
  255.6 179.3 %all-reduce.11.cloned.1.call-done = f32[1,1024,128]{1,2,0:T(8,128)} async-done(((f32[1,1024,128]{1,2,0:T(8,128)}), f32[1,1024,128]{1,2,0:T(8,128)}) %all-reduce.11.cloned.1.call-update) | async-done | bytes 524304 | tf_op jit(solution)/shard_map/psum | solution.py:45
  435.0 1.6 fusion.11
  437.3 11.7 custom-call.20
  450.4 9.8 custom-call.21
  461.5 1.0 convolution_bitcast_fusion.10
  462.8 1.5 fusion.5
  464.7 1.0 fusion.43
  465.7 179.1 %all-reduce.13.cloned.1.call-done = f32[1,1024,128]{1,2,0:T(8,128)} async-done(((f32[1,1024,128]{1,2,0:T(8,128)}), f32[1,1024,128]{1,2,0:T(8,128)}) %all-reduce.13.cloned.1.call-update) | async-done | bytes 524304 | tf_op jit(solution)/shard_map/psum | solution.py:45
  644.8 1.6 fusion.13
  647.2 11.7 custom-call.22
  660.2 9.8 custom-call.23
  672.6 1.5 fusion.4
  674.3 1.0 fusion.30
  675.3 179.4 %all-reduce.15.cloned.1.call-done = f32[1,1024,128]{1,2,0:T(8,128)} async-done(((f32[1,1024,128]{1,2,0:T(8,128)}), f32[1,1024,128]{1,2,0:T(8,128)}) %all-reduce.15.cloned.1.call-update) | async-done | bytes 524304 | tf_op jit(solution)/shard_map/psum | solution.py:45
  854.8 1.6 fusion.15
  857.1 11.7 custom-call.24
  870.1 9.8 custom-call.25
  881.3 1.0 convolution_bitcast_fusion.9
  882.5 1.5 fusion.3
  884.3 1.0 fusion.40
  885.3 179.3 %all-reduce.17.cloned.1.call-done = f32[1,1024,128]{1,2,0:T(8,128)} async-done(((f32[1,1024,128]{1,2,0:T(8,128)}), f32[1,1024,128]{1,2,0:T(8,128)}) %all-reduce.17.cloned.1.call-update) | async-done | bytes 524304 | tf_op jit(solution)/shard_map/psum | solution.py:45
  1064.6 1.6 fusion.17
  1067.0 11.7 custom-call.26
  1080.0 9.8 custom-call.27
  1092.4 1.5 fusion.2
  1095.3 179.1 %all-reduce.19.cloned.1.call-done = f32[1,1024,128]{1,2,0:T(8,128)} async-done(((f32[1,1024,128]{1,2,0:T(8,128)}), f32[1,1024,128]{1,2,0:T(8,128)}) %all-reduce.19.cloned.1.call-update) | async-done | bytes 524304 | tf_op jit(solution)/shard_map/psum | solution.py:45
  1274.5 1.6 fusion.19
  1276.8 11.7 custom-call.28
  1289.9 9.8 custom-call.29
  1302.3 1.5 fusion.1
  1305.0 179.4 %all-reduce.21.cloned.1.call-done = f32[1,1024,128]{1,2,0:T(8,128)} async-done(((f32[1,1024,128]{1,2,0:T(8,128)}), f32[1,1024,128]{1,2,0:T(8,128)}) %all-reduce.21.cloned.1.call-update) | async-done | bytes 524304 | tf_op jit(solution)/shard_map/psum | solution.py:45
  1484.4 1.6 fusion.21
  1486.7 11.7 custom-call.30
  1499.8 9.8 custom-call.31
  1512.1 1.5 fusion
  1515.5 178.8 %all-reduce.23.cloned.1.call-done = f32[1,1024,128]{1,2,0:T(8,128)} async-done(((f32[1,1024,128]{1,2,0:T(8,128)}), f32[1,1024,128]{1,2,0:T(8,128)}) %all-reduce.23.cloned.1.call-update) | async-done | bytes 524304 | tf_op jit(solution)/shard_map/psum | solution.py:45
  1694.3 1.6 fusion.22
  (103 shorter events, 39.1 us)
Async XLA Ops:
  7.2 29.9 %copy-start = (f32[1,1,1024,128]{3,2,1,0:T(8,128)S(1)}, f32[1,1,1024,128]{3,2,1,0:T(8,128)}, u32[]{:S(2)}) copy-start(f32[1,1,1024,128]{3,2,1,0:T(8,128)} %param.11) | copy-start | bytes 1572868
  7.2 217.9 %all-reduce.9.cloned.1.call-start = ((), (), s32[]{:S(2)}) async-start(), calls=%async_computation | async-start | bytes 1048576 | tf_op jit(solution)/shard_map/psum | solution.py:45
  7.9 14.0 copy-start.5
  7.9 26.8 %copy-start.3 = (f32[1,1024,128]{2,1,0:T(8,128)S(1)}, f32[1,1024,128]{2,1,0:T(8,128)}, u32[]{:S(2)}) copy-start(f32[1,1024,128]{2,1,0:T(8,128)} %param.18) | copy-start | bytes 1572868
  34.7 1.0 copy-start.4
  38.5 1.0 copy-start.2
  38.5 186.5 %copy-start.1 = (f32[1,1024,128]{2,1,0:T(8,128)S(1)}, f32[1,1024,128]{2,1,0:T(8,128)}, u32[]{:S(2)}) copy-start(f32[1,1024,128]{2,1,0:T(8,128)} %param.16) | copy-start | bytes 1572868
  38.6 396.4 %all-reduce.11.cloned.1.call-start = ((), (), s32[]{:S(2)}) async-start(), calls=%async_computation.1 | async-start | bytes 1048576 | tf_op jit(solution)/shard_map/psum | solution.py:45
  254.4 390.4 %all-reduce.13.cloned.1.call-start = ((), (), s32[]{:S(2)}) async-start(), calls=%async_computation.2 | async-start | bytes 1048576 | tf_op jit(solution)/shard_map/psum | solution.py:45
  464.2 390.5 %all-reduce.15.cloned.1.call-start = ((), (), s32[]{:S(2)}) async-start(), calls=%async_computation.3 | async-start | bytes 1048576 | tf_op jit(solution)/shard_map/psum | solution.py:45
  674.1 390.6 %all-reduce.17.cloned.1.call-start = ((), (), s32[]{:S(2)}) async-start(), calls=%async_computation.4 | async-start | bytes 1048576 | tf_op jit(solution)/shard_map/psum | solution.py:45
  884.0 390.5 %all-reduce.19.cloned.1.call-start = ((), (), s32[]{:S(2)}) async-start(), calls=%async_computation.5 | async-start | bytes 1048576 | tf_op jit(solution)/shard_map/psum | solution.py:45
  1093.9 390.5 %all-reduce.21.cloned.1.call-start = ((), (), s32[]{:S(2)}) async-start(), calls=%async_computation.6 | async-start | bytes 1048576 | tf_op jit(solution)/shard_map/psum | solution.py:45
  1303.8 390.5 %all-reduce.23.cloned.1.call-start = ((), (), s32[]{:S(2)}) async-start(), calls=%async_computation.7 | async-start | bytes 1048576 | tf_op jit(solution)/shard_map/psum | solution.py:45
Sparse Core Ops, SparseCore 0:
  38.7 186.3 all-reduce.8
  254.5 180.4 all-reduce.10
  464.4 180.4 all-reduce.12
  674.2 180.4 all-reduce.14
  884.1 180.4 all-reduce.16
  1094.0 180.4 all-reduce.18
  1303.9 180.4 all-reduce.20
  1513.8 180.4 all-reduce.22
where the time goes:
time: 1710 us; the launch traced here: 1700 us
  waiting for transfers between devices  1440 us (84%)
  other arithmetic  161 us (9%)
  matrix products  56.9 us (3%)
  blocking collectives  26.8 us (2%)
    psum x8, waiting for transfers between devices, combine(): total = lax.psum(partial_value, 'past')  1440 us
    another operation x21, other arithmetic, lower_inverse(): lower = jnp.linalg.cholesky(gram)  86.7 us
    another operation x14, other arithmetic, lower_inverse(): jax.scipy.linalg.solve_triangular(one, ident, lower=True)  73.3 us
  transfers between devices with their start and end apart: 8, of which 8 were waited for; matrix products, arithmetic and copies ran while one was open for 1% of the time, Pallas kernels for 0%

commit v1 on v0

--- a/solution.py
+++ b/solution.py
@@ -42,7 +42,7 @@
 
     def combine(terms, orthogonal):
         partial_value, vectors, small = terms
-        total = lax.psum(partial_value, "past")
+        total = jnp.sum(lax.all_gather(partial_value, "past"), axis=0)
         total = total + jnp.einsum("ibr,irt->ibt", vectors, small, precision=HIGH)
         if orthogonal:
             gram = jnp.einsum("ibr,ibs->irs", total, total, precision=HIGH)

time: 1710 us -> 1560 us (0.912)
  waiting for transfers between devices: 1440 us -> 1110 us
  local copies, waits for them, and re-layouts: 2.46 us -> 120 us
  other arithmetic: 161 us -> 236 us
    psum x8 -> x0, waiting for transfers between devices: 1440 us -> none  [combine(): total = lax.psum(partial_value, 'past')]
    all_gather x0 -> x8, waiting for transfers between devices: none -> 1110 us  [combine(): total = jnp.sum(lax.all_gather(partial_value, 'past'), axis=0)]
    unnamed x13 -> x11, local copies, waits for them, and re-layouts: 1.84 us -> 115 us
    reduce_sum x0 -> x8, other arithmetic: none -> 74.8 us  [combine(): total = jnp.sum(lax.all_gather(partial_value, 'past'), axis=0)]
where the time goes in v1:
time: 1560 us; the launch traced here: 1550 us
  waiting for transfers between devices  1110 us (71%)
  other arithmetic  236 us (15%)
  local copies, waits for them, and re-layouts  120 us (8%)
  matrix products  48.7 us (3%)
  blocking collectives  26.9 us (2%)
  between operations  16 us (1%)
    all_gather x8, waiting for transfers between devices, combine(): total = jnp.sum(lax.all_gather(partial_value, 'past'), axis=0)  1110 us
    unnamed x11, local copies, waits for them, and re-layouts  115 us
    another operation x21, other arithmetic, lower_inverse(): lower = jnp.linalg.cholesky(gram)  86.7 us
    reduce_sum x8, other arithmetic, combine(): total = jnp.sum(lax.all_gather(partial_value, 'past'), axis=0)  74.8 us
    another operation x14, other arithmetic, lower_inverse(): jax.scipy.linalg.solve_triangular(one, ident, lower=True)  73.3 us
  transfers between devices with their start and end apart: 8, of which 8 were waited for; matrix products, arithmetic and copies ran while one was open for 1% of the time, Pallas kernels for 0%

profile of v1, /device:TPU:8, one launch (start us, length us, event | category | flops | bytes accessed | tf_op | source)
XLA Modules:
  0.0 1553.2 jit_solution(2411524382220462764)
XLA Ops:
  7.9 13.9 all_gather.55
  21.8 13.0 all_gather.54
  34.8 2.0 convolution_bitcast_fusion.11
  36.8 2.0 fusion.17
  39.2 1.5 fusion.7
  40.7 2.2 fusion.40
  42.9 142.4 %all-gather.17.cloned.1.call-done = f32[65536,128]{0,1:T(8,128)} async-done(((f32[1024,128]{0,1:T(8,128)}), f32[65536,128]{0,1:T(8,128)}) %all-gather.17.cloned.1.call-update) | async-done | bytes 33554448 | tf_op jit(solution)/shard_map/all_gather | solution.py:45
  185.3 28.2 %copy.74 = f32[16,8,64,1024]{3,2,1,0:T(8,128)S(1)} copy(f32[16,8,64,1024]{3,1,2,0:T(8,128)} %bitcast.353) | data formatting | bytes 67108864
  213.5 7.2 bitcast_reduce_fusion.3
  222.1 11.7 custom-call.18
  235.1 9.8 custom-call.19
  246.2 1.0 fusion.51
  249.2 1.0 fusion.27
  250.2 137.7 %all-gather.19.cloned.1.call-done = f32[64,1024,128]{2,1,0:T(8,128)} async-done(((f32[1,1024,128]{2,1,0:T(8,128)}), f32[64,1024,128]{2,1,0:T(8,128)}) %all-gather.19.cloned.1.call-update) | async-done | bytes 33554448 | tf_op jit(solution)/shard_map/all_gather | solution.py:45
  388.0 11.9 reduce.16
  401.4 11.7 custom-call.20
  414.4 9.8 custom-call.21
  426.8 1.5 fusion.5
  428.4 1.0 fusion.37
  429.4 137.7 %all-gather.21.cloned.1.call-done = f32[65536,128]{0,1:T(8,128)} async-done(((f32[1024,128]{0,1:T(8,128)}), f32[65536,128]{0,1:T(8,128)}) %all-gather.21.cloned.1.call-update) | async-done | bytes 33554448 | tf_op jit(solution)/shard_map/all_gather | solution.py:45
  567.0 28.6 %copy.75 = f32[16,8,64,1024]{3,2,1,0:T(8,128)S(1)} copy(f32[16,8,64,1024]{3,1,2,0:T(8,128)} %bitcast.350) | data formatting | bytes 67108864
  595.6 6.7 bitcast_reduce_fusion.2
  603.6 11.7 custom-call.22
  616.7 9.8 custom-call.23
  627.8 1.0 fusion.48
  630.8 1.0 fusion.24
  631.8 137.7 %all-gather.23.cloned.1.call-done = f32[64,1024,128]{2,1,0:T(8,128)} async-done(((f32[1,1024,128]{2,1,0:T(8,128)}), f32[64,1024,128]{2,1,0:T(8,128)}) %all-gather.23.cloned.1.call-update) | async-done | bytes 33554448 | tf_op jit(solution)/shard_map/all_gather | solution.py:45
  769.5 11.9 reduce.18
  782.9 11.7 custom-call.24
  796.0 9.8 custom-call.25
  808.4 1.5 fusion.3
  810.9 137.7 %all-gather.25.cloned.1.call-done = f32[65536,128]{0,1:T(8,128)} async-done(((f32[1024,128]{0,1:T(8,128)}), f32[65536,128]{0,1:T(8,128)}) %all-gather.25.cloned.1.call-update) | async-done | bytes 33554448 | tf_op jit(solution)/shard_map/all_gather | solution.py:45
  948.6 28.6 %copy.76 = f32[16,8,64,1024]{3,2,1,0:T(8,128)S(1)} copy(f32[16,8,64,1024]{3,1,2,0:T(8,128)} %bitcast.351) | data formatting | bytes 67108864
  977.2 6.7 bitcast_reduce_fusion.1
  985.2 11.7 custom-call.26
  998.2 9.8 custom-call.27
  1013.4 137.7 %all-gather.27.cloned.1.call-done = f32[64,1024,128]{2,1,0:T(8,128)} async-done(((f32[1,1024,128]{2,1,0:T(8,128)}), f32[64,1024,128]{2,1,0:T(8,128)}) %all-gather.27.cloned.1.call-update) | async-done | bytes 33554448 | tf_op jit(solution)/shard_map/all_gather | solution.py:45
  1151.1 11.9 reduce.20
  1164.5 11.7 custom-call.28
  1177.5 9.8 custom-call.29
  1189.9 1.5 fusion.1
  1192.5 137.7 %all-gather.29.cloned.1.call-done = f32[65536,128]{0,1:T(8,128)} async-done(((f32[1024,128]{0,1:T(8,128)}), f32[65536,128]{0,1:T(8,128)}) %all-gather.29.cloned.1.call-update) | async-done | bytes 33554448 | tf_op jit(solution)/shard_map/all_gather | solution.py:45
  1330.1 28.2 %copy.77 = f32[16,8,64,1024]{3,2,1,0:T(8,128)S(1)} copy(f32[16,8,64,1024]{3,1,2,0:T(8,128)} %bitcast.352) | data formatting | bytes 67108864
  1358.3 6.9 bitcast_reduce_fusion
  1366.6 11.7 custom-call.30
  1379.6 9.8 custom-call.31
  1395.5 136.9 %all-gather.31.cloned.1.call-done = f32[64,1024,128]{2,1,0:T(8,128)} async-done(((f32[1,1024,128]{2,1,0:T(8,128)}), f32[64,1024,128]{2,1,0:T(8,128)}) %all-gather.31.cloned.1.call-update) | async-done | bytes 33554448 | tf_op jit(solution)/shard_map/all_gather | solution.py:45
  1532.5 11.7 reduce.22
  (117 shorter events, 48.8 us)
Async XLA Ops:
  7.2 32.0 %copy-start = (f32[1,1,1024,128]{3,2,1,0:T(8,128)S(1)}, f32[1,1,1024,128]{3,2,1,0:T(8,128)}, u32[]{:S(2)}) copy-start(f32[1,1,1024,128]{3,2,1,0:T(8,128)} %param.11) | copy-start | bytes 1572868
  7.2 178.1 %all-gather.17.cloned.1.call-start = ((), (), s32[]{:S(2)}) async-start(), calls=%async_computation | async-start | bytes 34078720 | tf_op jit(solution)/shard_map/all_gather | solution.py:45
  40.6 347.3 %all-gather.19.cloned.1.call-start = ((), (), s32[]{:S(2)}) async-start(), calls=%async_computation.1 | async-start | bytes 34078720 | tf_op jit(solution)/shard_map/all_gather | solution.py:45
  213.5 7.2 copy-start.1
  213.5 186.5 %copy-start.2 = (f32[1,1024,128]{2,1,0:T(8,128)S(1)}, f32[1,1024,128]{2,1,0:T(8,128)}, u32[]{:S(2)}) copy-start(f32[1,1024,128]{2,1,0:T(8,128)} %param.17) | copy-start | bytes 1572868
  249.2 317.8 %all-gather.21.cloned.1.call-start = ((), (), s32[]{:S(2)}) async-start(), calls=%async_computation.2 | async-start | bytes 34078720 | tf_op jit(solution)/shard_map/all_gather | solution.py:45
  428.3 341.2 %all-gather.23.cloned.1.call-start = ((), (), s32[]{:S(2)}) async-start(), calls=%async_computation.3 | async-start | bytes 34078720 | tf_op jit(solution)/shard_map/all_gather | solution.py:45
  630.8 317.8 %all-gather.25.cloned.1.call-start = ((), (), s32[]{:S(2)}) async-start(), calls=%async_computation.4 | async-start | bytes 34078720 | tf_op jit(solution)/shard_map/all_gather | solution.py:45
  809.9 341.2 %all-gather.27.cloned.1.call-start = ((), (), s32[]{:S(2)}) async-start(), calls=%async_computation.5 | async-start | bytes 34078720 | tf_op jit(solution)/shard_map/all_gather | solution.py:45
  1012.3 317.8 %all-gather.29.cloned.1.call-start = ((), (), s32[]{:S(2)}) async-start(), calls=%async_computation.6 | async-start | bytes 34078720 | tf_op jit(solution)/shard_map/all_gather | solution.py:45
  1191.4 341.1 %all-gather.31.cloned.1.call-start = ((), (), s32[]{:S(2)}) async-start(), calls=%async_computation.7 | async-start | bytes 34078720 | tf_op jit(solution)/shard_map/all_gather | solution.py:45
Sparse Core Ops, SparseCore 0:
  40.8 144.4 all-gather.16
  249.3 138.6 all-gather.18
  428.4 138.5 all-gather.20
  630.9 138.6 all-gather.22
  810.0 138.5 all-gather.24
  1012.4 138.6 all-gather.26
  1191.5 138.5 all-gather.28
  1393.8 138.6 all-gather.30
